TPU v7x, 256 devices: a whole 4x4x8 slice. The times are simulated.
256 devices in a mesh: leaf: 16 (over y, x), sep: 8 (over z), mode: 2 (over core).
Axes of the slice: x: 4, y: 4, z: 8, core: 2. Of those that a mesh axis runs over, the one named last changes fastest.
Arguments:
- modes: bfloat16 [1024, 2048, 256], P(('leaf', 'sep'), 'mode'), may hold values from -0.125 to 0.125
- coupling: bfloat16 [1024, 2048, 256], P(('leaf', 'sep'), 'mode'), may hold values from -6 to 6
- eigenvalues: float32 [1024, 256], P(('leaf', 'sep'), 'mode'), may hold values from 200 to 4000
- separator_of: int32 [1024, 1], P(('leaf', 'sep')), may hold values from 0 to 7; in each aligned block of 8 rows (0 to 7, 8 to 15, ...) at most 2 rows name the same one
- row_offset: int32 [1024], P(('leaf', 'sep')), may hold values from 0 to 256
- stiffness: bfloat16 [8, 512, 512], P('sep', None, ('leaf', 'mode')), may hold values from -1 to 40
- start_block: bfloat16 [8, 512, 256], P('sep', ('leaf', 'mode')), may hold values from -40 to 40
- rotations: bfloat16 [8, 2, 256, 256], P('sep'), may hold values from -0.375 to 0.375
Outputs:
- subspace: bfloat16 [8, 512, 256], P('sep', ('leaf', 'mode'))
- column_norms: float32 [8, 2, 256], P('sep')
Inputs may be any that keep to these rules, and one draw needn't show every extreme that they name: `separator_of`: among the 8 leaves of one device at most 2 couple to one separator, and in every draw some separator gets exactly 2 of them.
All inputs are finite; a program needn't handle non-finite values.
Results may differ from a plain program's by a relative error of at most 0.0075.
Values may be sent and summed in bfloat16 or wider, within the bound.
No kernel may reach another device: no remote copies, remote signals or barrier semaphores. Data moves between devices by JAX's collectives and lax.ppermute only.
A program may use at most 64 MiB of HBM per device.

v0:
```python
import jax
import jax.numpy as jnp
from jax import lax
from jax.sharding import PartitionSpec as P

SEP_ROWS = 512
CAP = 2
ITERS = 2
epsilon = 1e-06


def leaf_projection(modes, coupling, eigenvalues):
    summed = lax.psum_scatter(
        jnp.einsum("ldm,ldw->mlw", modes, coupling, preferred_element_type=jnp.float32),
        "mode",
        scatter_dimension=0,
        tiled=True,
    )
    return (summed / jnp.sqrt(eigenvalues.T)[:, :, None]).astype(jnp.bfloat16)


def route_blocks(scaled, separator_of, row_offset):
    groups = lax.axis_size("sep")
    leaves = scaled.shape[1]
    target = separator_of[:, 0]
    leaf_order = jnp.arange(leaves)
    earlier = (target[:, None] == target[None, :]) & (leaf_order[None, :] < leaf_order[:, None])
    position = jnp.sum(earlier.astype(jnp.int32), 1)
    slot_of = target * CAP + position
    slot_table = slot_of[None, :] == jnp.arange(groups * CAP)[:, None]
    send_blocks = jnp.einsum(
        "sl,mlw->smw", slot_table.astype(jnp.bfloat16), scaled, preferred_element_type=jnp.float32
    ).astype(jnp.bfloat16)
    send_offsets = jnp.sum(jnp.where(slot_table, row_offset[None, :], 0), 1)
    block_shape = (groups, CAP, send_blocks.shape[1], send_blocks.shape[2])
    got_blocks, got_offsets = (
        lax.all_to_all(
            send_blocks.reshape(block_shape), "sep", split_axis=0, concat_axis=0, tiled=True
        ),
        lax.all_to_all(
            send_offsets.reshape(groups, CAP), "sep", split_axis=0, concat_axis=0, tiled=True
        ),
    )
    return (
        got_blocks.reshape(groups * CAP, block_shape[2], block_shape[3]),
        got_offsets.reshape(groups * CAP),
    )


def coupled_correction(full_block, blocks, offsets):
    width_rows = blocks.shape[2]

    def add_slot(slot_index, accumulated):
        offset = offsets[slot_index]
        weights = blocks[slot_index]
        window = lax.dynamic_slice_in_dim(full_block, offset, width_rows, 0)
        projected = jnp.dot(weights, window, preferred_element_type=jnp.float32).astype(
            jnp.bfloat16
        )
        update = jnp.einsum("mw,mc->wc", weights, projected, preferred_element_type=jnp.float32)
        current = lax.dynamic_slice_in_dim(accumulated, offset, width_rows, 0)
        return lax.dynamic_update_slice_in_dim(accumulated, current + update, offset, 0)

    initial = jnp.zeros(full_block.shape, jnp.float32)
    return lax.fori_loop(0, blocks.shape[0], add_slot, initial)


def gather_rows(own_block):
    return lax.all_gather(own_block, ("leaf", "mode"), axis=0, tiled=True)


def per_device(
    modes, coupling, eigenvalues, separator_of, row_offset, stiffness, start_block, rotations
):
    scaled = leaf_projection(modes, coupling, eigenvalues)
    blocks, offsets = route_blocks(scaled, separator_of, row_offset)
    stiff_columns = stiffness[0]
    own_block = start_block[0]
    ritz_turns = rotations[0]
    own_rows = own_block.shape[0]
    norm_list = []
    for iteration in range(ITERS):
        full_block = gather_rows(own_block)
        correction = coupled_correction(full_block, blocks, offsets)

        def assemble_rows(first_row, row_count, block_now=own_block, correction_now=correction):
            product = jnp.dot(stiff_columns, block_now, preferred_element_type=jnp.float32)
            return product - correction_now

        summed = lax.psum_scatter(
            assemble_rows(jnp.int32(0), lax.axis_size(("leaf", "mode")) * own_rows),
            ("leaf", "mode"),
            scatter_dimension=0,
            tiled=True,
        )
        squares = lax.psum(jnp.sum(summed * summed, 0), ("leaf", "mode"))
        column_scale = jnp.sqrt(squares / SEP_ROWS + epsilon)
        normed = (summed / column_scale).astype(jnp.bfloat16)
        own_block = jnp.dot(
            normed, ritz_turns[iteration], preferred_element_type=jnp.float32
        ).astype(jnp.bfloat16)
        norm_list.append(column_scale)
    return (own_block[None], jnp.stack(norm_list)[None])


def solution(mesh):
    in_specs = (
        P(("leaf", "sep"), "mode", None),
        P(("leaf", "sep"), "mode", None),
        P(("leaf", "sep"), "mode"),
        P(("leaf", "sep"), None),
        P(("leaf", "sep")),
        P("sep", None, ("leaf", "mode")),
        P("sep", ("leaf", "mode"), None),
        P("sep", None, None, None),
    )
    out_specs = (P("sep", ("leaf", "mode"), None), P("sep", None, None))
    return jax.shard_map(
        per_device, mesh=mesh, in_specs=in_specs, out_specs=out_specs, check_vma=False
    )
```

profile of v0, /device:TPU:1, one launch (start us, length us, event | category | flops | bytes accessed | tf_op | source)
XLA Modules:
  0.0 560.8 jit_solution(13401757239637969915)
XLA Ops:
  7.3 6.2 %convolution_bitcast_fusion = f32[256,8,256]{0,2,1:T(8,128)} fusion(bf16[8,1024,256]{2,1,0:T(8,128)(2,1)} %param.13, bf16[8,1024,256]{2,1,0:T(8,128)(2,1)} %param.12), kind=kOutput, calls=%fused_computation.13 | convolution fusion | flops 1073741824 | bytes 10485760 | tf_op jit(solution)/shard_map/ldm,ldw->mlw/dot_general | solution.py:14
  13.8 0.7 all_to_all.9
  14.5 9.0 %all-to-all-start = ((s32[8,1,2]{2,1,0:T(1,128)}), s32[8,1,2]{2,1,0:T(1,128)S(1)}, u32[]{:S(2)}, u32[]{:S(2)}) async-start(s32[8,1,2]{2,1,0:T(1,128)} %bitcast.7), calls=%async_computation | async-start | bytes 8192 | tf_op jit(solution)/shard_map/all_to_all | solution.py:40
  23.5 9.3 %reduce-scatter.6.cloned.1.call-done = f32[128,8,256]{0,2,1:T(8,128)} async-done(((f32[256,8,256]{0,2,1:T(8,128)}), f32[128,8,256]{0,2,1:T(8,128)}) %reduce-scatter.6.cloned.1.call-update) | async-done | bytes 1048592 | tf_op jit(solution)/shard_map/reduce_scatter | solution.py:13
  32.8 1.3 divide_convert_fusion
  35.5 1.8 copy.30
  37.3 6.8 %all-to-all-start.1 = ((bf16[8,2,128,256]{3,1,2,0:T(2,128)(2,1)}), bf16[8,2,128,256]{3,1,2,0:T(2,128)(2,1)S(1)}, u32[]{:S(2)}, u32[]{:S(2)}) async-start(bf16[8,2,128,256]{3,1,2,0:T(2,128)(2,1)} %copy.30), calls=%async_computation.2 | async-start | bytes 2097152 | tf_op jit(solution)/shard_map/all_to_all | solution.py:37
  44.2 25.3 %all-gather = bf16[1,512,256]{2,1,0:T(8,128)(2,1)S(1)} all-gather(bf16[1,16,256]{2,1,0:T(8,128)(2,1)S(1)} %copy-done.1), channel_id=2, replica_groups=mesh['leaf'=16,'sep'=8,'mode'=2] {'leaf','mode'}, dimensions={1}, use_global_device_ids=true | all-gather | bytes 270336 | tf_op jit(solution)/shard_map/all_gather | solution.py:69
  70.0 0.7 reduce.3
  70.8 2.6 all-to-all-done.1
  73.6 74.0 %while.26 = (s32[]{:T(128)}, f32[512,256]{1,0:T(8,128)S(1)}, s32[16]{0:T(128)S(1)}, bf16[16,128,256]{2,1,0:T(8,128)(2,1)S(1)}, bf16[512,256]{1,0:T(8,128)(2,1)S(1)}, /*index=5*/s32[]{:T(128)}, s32[]{:T(128)}, s32[]{:T(128)}) while((s32[]{:T(128)}, f32[512,256]{1,0:T(8,128)S(1)}, s32[16]{0:T(128)S(1)}, bf16[16,128,256]{2,1,0:T(8,128)(2,1)S(1)}, ...), condition=%wide.region_4.5_spmd, body=%wide.region_3.4_spmd.sunk | while | flops 33652740 | bytes 1312903 | solution.py:65
  73.6 0.6 dynamic_slice.92
  76.5 1.1 dynamic_update_slice.16
  77.7 0.6 dynamic_slice.92
  80.6 1.9 dynamic_update_slice.16
  82.5 0.6 dynamic_slice.92
  85.4 1.9 dynamic_update_slice.16
  87.3 0.6 dynamic_slice.92
  90.2 1.9 dynamic_update_slice.16
  92.1 0.6 dynamic_slice.92
  95.0 1.3 dynamic_update_slice.16
  96.3 0.6 dynamic_slice.92
  99.3 1.9 dynamic_update_slice.16
  101.2 0.6 dynamic_slice.92
  104.1 1.9 dynamic_update_slice.16
  108.9 1.9 dynamic_update_slice.16
  113.7 1.1 dynamic_update_slice.16
  114.9 0.6 dynamic_slice.92
  117.8 1.9 dynamic_update_slice.16
  119.7 0.6 dynamic_slice.92
  122.6 1.8 dynamic_update_slice.16
  127.4 1.9 dynamic_update_slice.16
  132.2 1.1 dynamic_update_slice.16
  136.3 1.9 dynamic_update_slice.16
  141.1 1.7 dynamic_update_slice.16
  145.7 1.9 dynamic_update_slice.16
  147.7 1.1 convolution_subtract_fusion
  148.8 80.6 %reduce-scatter.8.cloned.1.call-done = f32[16,256]{1,0:T(8,128)} async-done(((f32[512,256]{1,0:T(8,128)}), f32[16,256]{1,0:T(8,128)}) %reduce-scatter.8.cloned.1.call-update) | async-done | bytes 16400 | tf_op jit(solution)/shard_map/reduce_scatter | solution.py:90
  229.4 0.7 multiply_reduce_fusion.1
  230.1 64.6 %psum.14 = f32[256]{0:T(256)S(1)} all-reduce(f32[256]{0:T(256)S(1)} %multiply_reduce_fusion.1), channel_id=1, replica_groups=mesh['leaf'=16,'sep'=8,'mode'=2] {'leaf','mode'}, use_global_device_ids=true, to_apply=%region_7.8 | all-reduce | flops 256 | bytes 2048 | tf_op jit(solution)/shard_map/psum | solution.py:96
  294.7 0.9 convolution_convert_fusion.4
  295.6 22.6 %all_gather.7 = bf16[512,256]{1,0:T(8,128)(2,1)S(1)} all-gather(bf16[16,256]{1,0:T(8,128)(2,1)S(1)} %convolution_convert_fusion.4), channel_id=1, replica_groups=mesh['leaf'=16,'sep'=8,'mode'=2] {'leaf','mode'}, dimensions={0}, use_global_device_ids=true | all-gather | bytes 270336 | tf_op jit(solution)/shard_map/all_gather | solution.py:69
  318.3 85.1 %while.27 = (s32[]{:T(128)}, f32[512,256]{0,1:T(8,128)S(1)}, s32[16]{0:T(128)S(1)}, bf16[16,128,256]{2,1,0:T(8,128)(2,1)S(1)}, bf16[512,256]{1,0:T(8,128)(2,1)S(1)}, /*index=5*/s32[]{:T(128)}, s32[]{:T(128)}, s32[]{:T(128)}) while((s32[]{:T(128)}, f32[512,256]{0,1:T(8,128)S(1)}, s32[16]{0:T(128)S(1)}, bf16[16,128,256]{2,1,0:T(8,128)(2,1)S(1)}, ...), condition=%wide.region_9.10_spmd, body=%wide.region_8.9_spmd.sunk | while | flops 33652740 | bytes 2884751 | solution.py:65
  321.6 1.8 dynamic_update_slice.17
  326.8 1.9 dynamic_update_slice.17
  332.1 1.9 dynamic_update_slice.17
  337.4 1.9 dynamic_update_slice.17
  342.7 1.8 dynamic_update_slice.17
  347.9 1.9 dynamic_update_slice.17
  353.1 2.2 dynamic_update_slice.17
  358.7 1.9 dynamic_update_slice.17
  364.0 1.8 dynamic_update_slice.17
  369.2 1.9 dynamic_update_slice.17
  374.5 2.2 dynamic_update_slice.17
  380.1 1.9 dynamic_update_slice.17
  385.4 1.8 dynamic_update_slice.17
  390.6 1.9 dynamic_update_slice.17
  395.8 2.2 dynamic_update_slice.17
  401.4 1.9 dynamic_update_slice.17
  403.6 1.0 copy.34
  404.7 82.7 %reduce-scatter.10.cloned.1.call-done = f32[16,256]{1,0:T(8,128)} async-done(((f32[512,256]{1,0:T(8,128)}), f32[16,256]{1,0:T(8,128)}) %reduce-scatter.10.cloned.1.call-update) | async-done | bytes 16400
  487.3 0.8 copy.35
  488.2 64.6 %psum.15 = f32[256]{0:T(256)S(1)} all-reduce(f32[256]{0:T(256)S(1)} %multiply_reduce_fusion), channel_id=1, replica_groups=mesh['leaf'=16,'sep'=8,'mode'=2] {'leaf','mode'}, use_global_device_ids=true, to_apply=%region_12.13 | all-reduce | flops 256 | bytes 2048 | tf_op jit(solution)/shard_map/psum | solution.py:96
  552.8 0.9 fusion.17
  (139 shorter events, 35.4 us)
Async XLA Ops:
  7.2 140.5 %copy-start = (bf16[1,512,16]{1,2,0:T(8,128)(2,1)S(1)}, bf16[1,512,16]{1,2,0:T(8,128)(2,1)}, u32[]{:S(2)}) copy-start(bf16[1,512,16]{1,2,0:T(8,128)(2,1)} %param.17) | copy-start | bytes 49156
  7.2 6.3 %copy-start.4 = (s32[8,1]{0,1:T(1,128)S(1)}, s32[8,1]{0,1:T(1,128)}, u32[]{:S(2)}) copy-start(s32[8,1]{0,1:T(1,128)} %param.15) | copy-start | bytes 100
  7.2 6.5 %copy-start.5 = (s32[8]{0:T(128)S(1)}, s32[8]{0:T(128)}, u32[]{:S(2)}) copy-start(s32[8]{0:T(128)} %param.16) | copy-start | bytes 100
  7.2 16.3 %copy-start.2 = (f32[8,128]{1,0:T(8,128)S(1)}, f32[8,128]{1,0:T(8,128)}, u32[]{:S(2)}) copy-start(f32[8,128]{1,0:T(8,128)} %param.14) | copy-start | bytes 12292
  7.2 25.6 %reduce-scatter.6.cloned.1.call-start = ((), (), s32[]{:S(2)}) async-start(), calls=%async_computation.5 | async-start | bytes 3145728 | tf_op jit(solution)/shard_map/reduce_scatter | solution.py:13
  14.5 22.9 %all-to-all-start = ((s32[8,1,2]{2,1,0:T(1,128)}), s32[8,1,2]{2,1,0:T(1,128)S(1)}, u32[]{:S(2)}, u32[]{:S(2)}) async-start(s32[8,1,2]{2,1,0:T(1,128)} %bitcast.7), calls=%async_computation | async-start | bytes 8192 | tf_op jit(solution)/shard_map/all_to_all | solution.py:40
  34.5 9.6 %copy-start.1 = (bf16[1,16,256]{2,1,0:T(8,128)(2,1)S(1)}, bf16[1,16,256]{2,1,0:T(8,128)(2,1)}, u32[]{:S(2)}) copy-start(bf16[1,16,256]{2,1,0:T(8,128)(2,1)} %param.18) | copy-start | bytes 24580
  37.3 36.0 %all-to-all-start.1 = ((bf16[8,2,128,256]{3,1,2,0:T(2,128)(2,1)}), bf16[8,2,128,256]{3,1,2,0:T(2,128)(2,1)S(1)}, u32[]{:S(2)}, u32[]{:S(2)}) async-start(bf16[8,2,128,256]{3,1,2,0:T(2,128)(2,1)} %copy.30), calls=%async_computation.2 | async-start | bytes 2097152 | tf_op jit(solution)/shard_map/all_to_all | solution.py:37
  44.1 185.3 %reduce-scatter.8.cloned.1.call-start = ((), (), s32[]{:S(2)}) async-start(), calls=%async_computation.6 | async-start | bytes 540672 | tf_op jit(solution)/shard_map/reduce_scatter | solution.py:90
  73.6 221.1 %copy-start.3 = (bf16[1,2,256,256]{3,2,1,0:T(8,128)(2,1)S(1)}, bf16[1,2,256,256]{3,2,1,0:T(8,128)(2,1)}, u32[]{:S(2)}) copy-start(bf16[1,2,256,256]{3,2,1,0:T(8,128)(2,1)} %param.19) | copy-start | bytes 786436
  148.7 338.6 %reduce-scatter.10.cloned.1.call-start = ((), (), s32[]{:S(2)}) async-start(), calls=%async_computation.7 | async-start | bytes 540672
Sparse Core Ops, SparseCore 0:
  13.6 19.1 reduce-scatter.5
  148.9 80.5 reduce-scatter.7
  404.8 82.4 reduce-scatter.9
where the time goes:
time: 562 us; the launch traced here: 561 us
  blocking collectives  177 us (31%)
  waiting for transfers between devices  175 us (31%)
  local copies, waits for them, and re-layouts  89.7 us (16%)
  loops' own time  63.5 us (11%)
  matrix products  21.7 us (4%)
  starting transfers between devices  15.9 us (3%)
  between operations  13.9 us (2%)
    psum x2, blocking collectives, per_device(): squares = lax.psum(jnp.sum(summed * summed, 0), ('leaf', 'mode'))  129 us
    unnamed x4, waiting for transfers between devices  82.7 us
    reduce_scatter x1, waiting for transfers between devices, per_device(): lax.psum_scatter(assemble_rows(jnp.int32(0), lax.axis_size(('leaf', 'mode...  80.6 us
    another operation x2, loops' own time, coupled_correction(): return lax.fori_loop(0, blocks.shape[0], add_slot, initial)  63.5 us
    dynamic_update_slice x48, local copies, waits for them, and re-layouts, add_slot(): lax.dynamic_update_slice_in_dim(accumulated, current + update, offset, 0)  60.6 us
    all_gather x2, blocking collectives, gather_rows(): return lax.all_gather(own_block, ('leaf', 'mode'), axis=0, tiled=True)  48 us
    dynamic_slice x32, local copies, waits for them, and re-layouts, add_slot(): offset = offsets[slot_index]  18.8 us
    dot_general x32, matrix products, add_slot(): jnp.einsum('mw,mc->wc', weights, projected, preferred_element_type=jnp.fl...  11.9 us
  transfers between devices with their start and end apart: 5, of which 4 were waited for; matrix products, arithmetic and copies ran while one was open for 1% of the time, Pallas kernels for 0%

commit v1 on v0

--- a/solution.py
+++ b/solution.py
@@ -93,7 +93,7 @@
             scatter_dimension=0,
             tiled=True,
         )
-        squares = lax.psum(jnp.sum(summed * summed, 0), ("leaf", "mode"))
+        squares = lax.psum(lax.psum(jnp.sum(summed * summed, 0), "leaf"), "mode")
         column_scale = jnp.sqrt(squares / SEP_ROWS + epsilon)
         normed = (summed / column_scale).astype(jnp.bfloat16)
         own_block = jnp.dot(

time: 562 us -> 518 us (0.922)
  blocking collectives: 177 us -> 133 us
    psum x2 -> x4, blocking collectives: 129 us -> 85.5 us  [per_device(): squares = lax.psum(lax.psum(jnp.sum(summed * summed, 0), 'leaf'), 'mode')]
where the time goes in v1:
time: 518 us; the launch traced here: 517 us
  waiting for transfers between devices  175 us (34%)
  blocking collectives  133 us (26%)
  local copies, waits for them, and re-layouts  89.7 us (17%)
  loops' own time  63.5 us (12%)
  matrix products  21.7 us (4%)
  starting transfers between devices  15.9 us (3%)
  between operations  13.9 us (3%)
    psum x4, blocking collectives, per_device(): squares = lax.psum(lax.psum(jnp.sum(summed * summed, 0), 'leaf'), 'mode')  85.5 us
    unnamed x4, waiting for transfers between devices  82.7 us
    reduce_scatter x1, waiting for transfers between devices, per_device(): lax.psum_scatter(assemble_rows(jnp.int32(0), lax.axis_size(('leaf', 'mode...  80.6 us
    another operation x2, loops' own time, coupled_correction(): return lax.fori_loop(0, blocks.shape[0], add_slot, initial)  63.5 us
    dynamic_update_slice x48, local copies, waits for them, and re-layouts, add_slot(): lax.dynamic_update_slice_in_dim(accumulated, current + update, offset, 0)  60.6 us
    all_gather x2, blocking collectives, gather_rows(): return lax.all_gather(own_block, ('leaf', 'mode'), axis=0, tiled=True)  47.5 us
    dynamic_slice x32, local copies, waits for them, and re-layouts, add_slot(): offset = offsets[slot_index]  18.8 us
    dot_general x32, matrix products, add_slot(): jnp.einsum('mw,mc->wc', weights, projected, preferred_element_type=jnp.fl...  11.9 us
  transfers between devices with their start and end apart: 5, of which 4 were waited for; matrix products, arithmetic and copies ran while one was open for 1% of the time, Pallas kernels for 0%

profile of v1, /device:TPU:1, one launch (start us, length us, event | category | flops | bytes accessed | tf_op | source)
XLA Modules:
  0.0 516.6 jit_solution(5746448079535010161)
XLA Ops:
  7.3 6.2 %convolution_bitcast_fusion = f32[256,8,256]{0,2,1:T(8,128)} fusion(bf16[8,1024,256]{2,1,0:T(8,128)(2,1)} %param.13, bf16[8,1024,256]{2,1,0:T(8,128)(2,1)} %param.12), kind=kOutput, calls=%fused_computation.13 | convolution fusion | flops 1073741824 | bytes 10485760 | tf_op jit(solution)/shard_map/ldm,ldw->mlw/dot_general | solution.py:14
  13.8 0.7 all_to_all.9
  14.5 9.0 %all-to-all-start = ((s32[8,1,2]{2,1,0:T(1,128)}), s32[8,1,2]{2,1,0:T(1,128)S(1)}, u32[]{:S(2)}, u32[]{:S(2)}) async-start(s32[8,1,2]{2,1,0:T(1,128)} %bitcast.7), calls=%async_computation | async-start | bytes 8192 | tf_op jit(solution)/shard_map/all_to_all | solution.py:40
  23.5 9.3 %reduce-scatter.6.cloned.1.call-done = f32[128,8,256]{0,2,1:T(8,128)} async-done(((f32[256,8,256]{0,2,1:T(8,128)}), f32[128,8,256]{0,2,1:T(8,128)}) %reduce-scatter.6.cloned.1.call-update) | async-done | bytes 1048592 | tf_op jit(solution)/shard_map/reduce_scatter | solution.py:13
  32.8 1.3 divide_convert_fusion
  35.5 1.8 copy.30
  37.3 6.8 %all-to-all-start.1 = ((bf16[8,2,128,256]{3,1,2,0:T(2,128)(2,1)}), bf16[8,2,128,256]{3,1,2,0:T(2,128)(2,1)S(1)}, u32[]{:S(2)}, u32[]{:S(2)}) async-start(bf16[8,2,128,256]{3,1,2,0:T(2,128)(2,1)} %copy.30), calls=%async_computation.2 | async-start | bytes 2097152 | tf_op jit(solution)/shard_map/all_to_all | solution.py:37
  44.2 25.3 %all-gather = bf16[1,512,256]{2,1,0:T(8,128)(2,1)S(1)} all-gather(bf16[1,16,256]{2,1,0:T(8,128)(2,1)S(1)} %copy-done.1), channel_id=2, replica_groups=mesh['leaf'=16,'sep'=8,'mode'=2] {'leaf','mode'}, dimensions={1}, use_global_device_ids=true | all-gather | bytes 270336 | tf_op jit(solution)/shard_map/all_gather | solution.py:69
  70.0 0.7 reduce.3
  70.8 2.6 all-to-all-done.1
  73.6 74.0 %while.26 = (s32[]{:T(128)}, f32[512,256]{1,0:T(8,128)S(1)}, s32[16]{0:T(128)S(1)}, bf16[16,128,256]{2,1,0:T(8,128)(2,1)S(1)}, bf16[512,256]{1,0:T(8,128)(2,1)S(1)}, /*index=5*/s32[]{:T(128)}, s32[]{:T(128)}, s32[]{:T(128)}) while((s32[]{:T(128)}, f32[512,256]{1,0:T(8,128)S(1)}, s32[16]{0:T(128)S(1)}, bf16[16,128,256]{2,1,0:T(8,128)(2,1)S(1)}, ...), condition=%wide.region_4.5_spmd, body=%wide.region_3.4_spmd.sunk | while | flops 33652740 | bytes 1312903 | solution.py:65
  73.6 0.6 dynamic_slice.92
  76.5 1.1 dynamic_update_slice.16
  77.7 0.6 dynamic_slice.92
  80.6 1.9 dynamic_update_slice.16
  82.5 0.6 dynamic_slice.92
  85.4 1.9 dynamic_update_slice.16
  87.3 0.6 dynamic_slice.92
  90.2 1.9 dynamic_update_slice.16
  92.1 0.6 dynamic_slice.92
  95.0 1.3 dynamic_update_slice.16
  96.3 0.6 dynamic_slice.92
  99.3 1.9 dynamic_update_slice.16
  101.2 0.6 dynamic_slice.92
  104.1 1.9 dynamic_update_slice.16
  108.9 1.9 dynamic_update_slice.16
  113.7 1.1 dynamic_update_slice.16
  117.8 1.9 dynamic_update_slice.16
  122.6 1.8 dynamic_update_slice.16
  127.4 1.9 dynamic_update_slice.16
  132.2 1.1 dynamic_update_slice.16
  136.3 1.9 dynamic_update_slice.16
  141.1 1.7 dynamic_update_slice.16
  145.7 1.9 dynamic_update_slice.16
  147.7 1.1 convolution_subtract_fusion
  148.8 80.6 %reduce-scatter.8.cloned.1.call-done = f32[16,256]{1,0:T(8,128)} async-done(((f32[512,256]{1,0:T(8,128)}), f32[16,256]{1,0:T(8,128)}) %reduce-scatter.8.cloned.1.call-update) | async-done | bytes 16400 | tf_op jit(solution)/shard_map/reduce_scatter | solution.py:90
  229.4 0.7 multiply_reduce_fusion.1
  230.1 30.9 %psum.28 = f32[256]{0:T(256)S(1)} all-reduce(f32[256]{0:T(256)S(1)} %multiply_reduce_fusion.1), channel_id=1, replica_groups=mesh['leaf'=16,'sep'=8,'mode'=2] {'leaf'}, use_global_device_ids=true, to_apply=%region_7.8 | all-reduce | flops 256 | bytes 2048 | tf_op jit(solution)/shard_map/psum | solution.py:96
  261.0 11.9 %psum.29 = f32[256]{0:T(256)S(1)} all-reduce(f32[256]{0:T(256)S(1)} %psum.28), channel_id=1, replica_groups=mesh['leaf'=16,'sep'=8,'mode'=2] {'mode'}, use_global_device_ids=true, to_apply=%region_8.9 | all-reduce | flops 256 | bytes 2048 | tf_op jit(solution)/shard_map/psum | solution.py:96
  272.9 0.9 convolution_convert_fusion.4
  273.8 22.1 %all_gather.7 = bf16[512,256]{1,0:T(8,128)(2,1)S(1)} all-gather(bf16[16,256]{1,0:T(8,128)(2,1)S(1)} %convolution_convert_fusion.4), channel_id=1, replica_groups=mesh['leaf'=16,'sep'=8,'mode'=2] {'leaf','mode'}, dimensions={0}, use_global_device_ids=true | all-gather | bytes 270336 | tf_op jit(solution)/shard_map/all_gather | solution.py:69
  296.0 85.1 %while.27 = (s32[]{:T(128)}, f32[512,256]{0,1:T(8,128)S(1)}, s32[16]{0:T(128)S(1)}, bf16[16,128,256]{2,1,0:T(8,128)(2,1)S(1)}, bf16[512,256]{1,0:T(8,128)(2,1)S(1)}, /*index=5*/s32[]{:T(128)}, s32[]{:T(128)}, s32[]{:T(128)}) while((s32[]{:T(128)}, f32[512,256]{0,1:T(8,128)S(1)}, s32[16]{0:T(128)S(1)}, bf16[16,128,256]{2,1,0:T(8,128)(2,1)S(1)}, ...), condition=%wide.region_10.11_spmd, body=%wide.region_9.10_spmd.sunk | while | flops 33652740 | bytes 2884751 | solution.py:65
  299.3 1.8 dynamic_update_slice.17
  304.5 1.9 dynamic_update_slice.17
  309.8 1.9 dynamic_update_slice.17
  315.1 1.9 dynamic_update_slice.17
  320.3 1.8 dynamic_update_slice.17
  325.5 1.9 dynamic_update_slice.17
  330.8 2.2 dynamic_update_slice.17
  336.4 1.9 dynamic_update_slice.17
  341.7 1.8 dynamic_update_slice.17
  346.9 1.9 dynamic_update_slice.17
  352.2 2.2 dynamic_update_slice.17
  357.8 1.9 dynamic_update_slice.17
  363.0 1.8 dynamic_update_slice.17
  368.2 1.9 dynamic_update_slice.17
  373.5 2.2 dynamic_update_slice.17
  379.1 1.9 dynamic_update_slice.17
  381.3 1.0 copy.34
  382.3 82.6 %reduce-scatter.10.cloned.1.call-done = f32[16,256]{1,0:T(8,128)} async-done(((f32[512,256]{1,0:T(8,128)}), f32[16,256]{1,0:T(8,128)}) %reduce-scatter.10.cloned.1.call-update) | async-done | bytes 16400
  465.0 0.8 copy.35
  465.9 30.9 %psum.30 = f32[256]{0:T(256)S(1)} all-reduce(f32[256]{0:T(256)S(1)} %multiply_reduce_fusion), channel_id=1, replica_groups=mesh['leaf'=16,'sep'=8,'mode'=2] {'leaf'}, use_global_device_ids=true, to_apply=%region_13.14 | all-reduce | flops 256 | bytes 2048 | tf_op jit(solution)/shard_map/psum | solution.py:96
  496.8 11.9 %psum.31 = f32[256]{0:T(256)S(1)} all-reduce(f32[256]{0:T(256)S(1)} %psum.30), channel_id=1, replica_groups=mesh['leaf'=16,'sep'=8,'mode'=2] {'mode'}, use_global_device_ids=true, to_apply=%region_14.15 | all-reduce | flops 256 | bytes 2048 | tf_op jit(solution)/shard_map/psum | solution.py:96
  508.6 0.9 fusion.17
  (141 shorter events, 36.6 us)
Async XLA Ops:
  7.2 140.5 %copy-start = (bf16[1,512,16]{1,2,0:T(8,128)(2,1)S(1)}, bf16[1,512,16]{1,2,0:T(8,128)(2,1)}, u32[]{:S(2)}) copy-start(bf16[1,512,16]{1,2,0:T(8,128)(2,1)} %param.17) | copy-start | bytes 49156
  7.2 6.3 %copy-start.4 = (s32[8,1]{0,1:T(1,128)S(1)}, s32[8,1]{0,1:T(1,128)}, u32[]{:S(2)}) copy-start(s32[8,1]{0,1:T(1,128)} %param.15) | copy-start | bytes 100
  7.2 6.5 %copy-start.5 = (s32[8]{0:T(128)S(1)}, s32[8]{0:T(128)}, u32[]{:S(2)}) copy-start(s32[8]{0:T(128)} %param.16) | copy-start | bytes 100
  7.2 16.3 %copy-start.2 = (f32[8,128]{1,0:T(8,128)S(1)}, f32[8,128]{1,0:T(8,128)}, u32[]{:S(2)}) copy-start(f32[8,128]{1,0:T(8,128)} %param.14) | copy-start | bytes 12292
  7.2 25.6 %reduce-scatter.6.cloned.1.call-start = ((), (), s32[]{:S(2)}) async-start(), calls=%async_computation.5 | async-start | bytes 3145728 | tf_op jit(solution)/shard_map/reduce_scatter | solution.py:13
  14.5 22.9 %all-to-all-start = ((s32[8,1,2]{2,1,0:T(1,128)}), s32[8,1,2]{2,1,0:T(1,128)S(1)}, u32[]{:S(2)}, u32[]{:S(2)}) async-start(s32[8,1,2]{2,1,0:T(1,128)} %bitcast.7), calls=%async_computation | async-start | bytes 8192 | tf_op jit(solution)/shard_map/all_to_all | solution.py:40
  34.5 9.6 %copy-start.1 = (bf16[1,16,256]{2,1,0:T(8,128)(2,1)S(1)}, bf16[1,16,256]{2,1,0:T(8,128)(2,1)}, u32[]{:S(2)}) copy-start(bf16[1,16,256]{2,1,0:T(8,128)(2,1)} %param.18) | copy-start | bytes 24580
  37.3 36.0 %all-to-all-start.1 = ((bf16[8,2,128,256]{3,1,2,0:T(2,128)(2,1)}), bf16[8,2,128,256]{3,1,2,0:T(2,128)(2,1)S(1)}, u32[]{:S(2)}, u32[]{:S(2)}) async-start(bf16[8,2,128,256]{3,1,2,0:T(2,128)(2,1)} %copy.30), calls=%async_computation.2 | async-start | bytes 2097152 | tf_op jit(solution)/shard_map/all_to_all | solution.py:37
  44.1 185.3 %reduce-scatter.8.cloned.1.call-start = ((), (), s32[]{:S(2)}) async-start(), calls=%async_computation.6 | async-start | bytes 540672 | tf_op jit(solution)/shard_map/reduce_scatter | solution.py:90
  73.6 199.3 %copy-start.3 = (bf16[1,2,256,256]{3,2,1,0:T(8,128)(2,1)S(1)}, bf16[1,2,256,256]{3,2,1,0:T(8,128)(2,1)}, u32[]{:S(2)}) copy-start(bf16[1,2,256,256]{3,2,1,0:T(8,128)(2,1)} %param.19) | copy-start | bytes 786436
  148.7 316.2 %reduce-scatter.10.cloned.1.call-start = ((), (), s32[]{:S(2)}) async-start(), calls=%async_computation.7 | async-start | bytes 540672
Sparse Core Ops, SparseCore 0:
  13.6 19.1 reduce-scatter.5
  148.9 80.5 reduce-scatter.7
  382.5 82.4 reduce-scatter.9
